TPU v7x, 128 devices: a whole 4x4x4 slice. The times are simulated.
128 devices in a mesh: req: 64 (over z_lo, x, y, core), kvh: 2 (over z_hi).
Axes of the slice: x: 4, y: 4, z: 4 (z_hi: 2, z_lo: 2; z = z_hi * 2 + z_lo), core: 2. Of those that a mesh axis runs over, the one named last changes fastest.
Arguments:
- queries: bfloat16 [64, 4, 8192], P('req', None, 'kvh'), may hold values from -42 to 42
- incoming_keys: bfloat16 [64, 4, 1024], P('req', None, 'kvh'), may hold values from -6 to 6
- incoming_values: bfloat16 [64, 4, 1024], P('req', None, 'kvh'), may hold values from -6 to 6
- system_prefix_keys: bfloat16 [8, 16384, 1024], P(None, 'req', 'kvh'), may hold values from -6 to 6
- system_prefix_values: bfloat16 [8, 16384, 1024], P(None, 'req', 'kvh'), may hold values from -6 to 6
- request_history_keys: bfloat16 [64, 2048, 1024], P('req', None, 'kvh'), may hold values from -6 to 6
- request_history_values: bfloat16 [64, 2048, 1024], P('req', None, 'kvh'), may hold values from -6 to 6
- kept: int32 [64, 8, 1024], P('req', 'kvh'), may hold values from 0 to 2047, as said below
- membership: int32 [64, 1], P('req'), may hold values from 0 to 7; in each aligned block of 64 rows (0 to 63, 64 to 127, ...) at most 16 rows name the same one
- out_weight: bfloat16 [8192, 8192], P('kvh', 'req'), may hold values from -0.0625 to 0.0625
Outputs:
- layer_out: bfloat16 [64, 4, 8192], P(None, None, 'req')
Inputs may be any that keep to these rules, and one draw needn't show every extreme that they name: `membership`: no system prompt has more than 16 requests; some prompt has exactly 16. `kept`: the 1024 positions of one request and KV head are distinct.
All inputs are finite; a program needn't handle non-finite values.
Results may differ from a plain program's by a relative error of at most 0.0049.
Values may be sent and summed in bfloat16 or wider, within the bound.
No kernel may reach another device: no remote copies, remote signals or barrier semaphores. Data moves between devices by JAX's collectives and lax.ppermute only.
A program may use at most 128 MiB of HBM per device.

v0:
```python
import jax
import jax.numpy as jnp
from jax import lax
from jax.sharding import PartitionSpec as P

HEAD_WIDTH = 128
HEADS_PER_GROUP = 8
PROMPT_COUNT = 8


def local_partial(scores):
    row_peak = jnp.max(scores, axis=-1)
    exp_terms = jnp.exp(scores - row_peak[..., None])
    row_total = jnp.sum(exp_terms, axis=-1)
    return (row_peak, row_total, exp_terms.astype(jnp.bfloat16))


def prefix_partials(
    query_all, member_all, system_prefix_keys, system_prefix_values, kv_local, score_scale
):
    total_rows, span_steps = (query_all.shape[0], query_all.shape[1])
    capacity = total_rows // 4
    stretch_len = system_prefix_keys.shape[1]
    member_ids = member_all[:, 0]
    onehot_table = member_ids[:, None] == jnp.arange(PROMPT_COUNT)[None, :]
    prompt_counts = jnp.sum(onehot_table.astype(jnp.int32), axis=0)
    prompt_starts = jnp.cumsum(prompt_counts) - prompt_counts
    sorted_order = jnp.argsort(member_ids, stable=True)
    grouped_query_heads = query_all.reshape(
        total_rows, span_steps, kv_local, HEADS_PER_GROUP, HEAD_WIDTH
    )
    peak_all = jnp.zeros((total_rows, span_steps, kv_local, HEADS_PER_GROUP), jnp.float32)
    total_all = jnp.zeros((total_rows, span_steps, kv_local, HEADS_PER_GROUP), jnp.float32)
    out_all = jnp.zeros(
        (total_rows, span_steps, kv_local, HEADS_PER_GROUP, HEAD_WIDTH), jnp.float32
    )
    slot_ids = jnp.arange(capacity)
    for prompt_id in range(PROMPT_COUNT):
        slot_pos = jnp.minimum(prompt_starts[prompt_id] + slot_ids, total_rows - 1)
        slot_rows = sorted_order[slot_pos]
        is_valid = (slot_ids < prompt_counts[prompt_id])[:, None, None, None]
        chosen_index = grouped_query_heads[slot_rows]
        stretch_keys = system_prefix_keys[prompt_id].reshape(stretch_len, kv_local, HEAD_WIDTH)
        stretch_values = system_prefix_values[prompt_id].reshape(stretch_len, kv_local, HEAD_WIDTH)
        scores = (
            jnp.einsum(
                "cskgd,lkd->cskgl", chosen_index, stretch_keys, preferred_element_type=jnp.float32
            )
            * score_scale
        )
        row_peak, row_total, weights = local_partial(scores)
        part_out = jnp.einsum(
            "cskgl,lkd->cskgd", weights, stretch_values, preferred_element_type=jnp.float32
        )
        peak_all = peak_all.at[slot_rows].add(jnp.where(is_valid, row_peak, 0.0))
        total_all = total_all.at[slot_rows].add(jnp.where(is_valid, row_total, 0.0))
        out_all = out_all.at[slot_rows].add(jnp.where(is_valid[..., None], part_out, 0.0))
    return (peak_all, total_all, out_all)


def return_partials(peak_all, total_all, out_all, req_rows):
    total_rows, span_steps, kv_local = (peak_all.shape[0], peak_all.shape[1], peak_all.shape[2])
    flat_peak = peak_all.reshape(total_rows, span_steps, kv_local * HEADS_PER_GROUP)
    flat_total = total_all.reshape(total_rows, span_steps, kv_local * HEADS_PER_GROUP)
    flat_out = out_all.reshape(total_rows, span_steps, kv_local * HEADS_PER_GROUP * HEAD_WIDTH)
    got_out, got_peak, got_total = (
        lax.all_to_all(flat_out, "req", split_axis=0, concat_axis=0, tiled=True),
        lax.all_to_all(flat_peak, "req", split_axis=0, concat_axis=0, tiled=True),
        lax.all_to_all(flat_total, "req", split_axis=0, concat_axis=0, tiled=True),
    )
    sources = total_rows // req_rows
    return (
        got_peak.reshape(sources, req_rows, span_steps, kv_local, HEADS_PER_GROUP),
        got_total.reshape(sources, req_rows, span_steps, kv_local, HEADS_PER_GROUP),
        got_out.reshape(sources, req_rows, span_steps, kv_local, HEADS_PER_GROUP, HEAD_WIDTH),
    )


def local(
    queries,
    incoming_keys,
    incoming_values,
    system_prefix_keys,
    system_prefix_values,
    request_history_keys,
    request_history_values,
    kept,
    membership,
    out_weight,
):
    req_rows, step_count, query_width = queries.shape
    kv_local = incoming_keys.shape[2] // HEAD_WIDTH
    score_scale = HEAD_WIDTH ** (-0.5)
    grouped_query_heads = queries.reshape(
        req_rows, step_count, kv_local, HEADS_PER_GROUP, HEAD_WIDTH
    )
    cache_keys = request_history_keys.reshape(req_rows, -1, kv_local, HEAD_WIDTH)
    cache_values = request_history_values.reshape(req_rows, -1, kv_local, HEAD_WIDTH)
    head_index_list = jnp.arange(kv_local)[None, :]
    retained_keys = jax.vmap(lambda key_table, pick_list: key_table[pick_list.T, head_index_list])(
        cache_keys, kept
    )
    retained_values = jax.vmap(
        lambda value_table, pick_list: value_table[pick_list.T, head_index_list]
    )(cache_values, kept)
    kept_scores = (
        jnp.einsum(
            "rtkgd,rlkd->rtkgl",
            grouped_query_heads,
            retained_keys,
            preferred_element_type=jnp.float32,
        )
        * score_scale
    )
    kept_peak, kept_total, kept_weights = local_partial(kept_scores)
    kept_out = jnp.einsum(
        "rtkgl,rlkd->rtkgd", kept_weights, retained_values, preferred_element_type=jnp.float32
    )
    recent_token_keys = incoming_keys.reshape(req_rows, step_count, kv_local, HEAD_WIDTH)
    recent_token_values = incoming_values.reshape(req_rows, step_count, kv_local, HEAD_WIDTH)
    fresh_scores = (
        jnp.einsum(
            "rtkgd,rukd->rtkgu",
            grouped_query_heads,
            recent_token_keys,
            preferred_element_type=jnp.float32,
        )
        * score_scale
    )
    causal_mask = jnp.arange(step_count)[None, :] <= jnp.arange(step_count)[:, None]
    fresh_scores = jnp.where(causal_mask[None, :, None, None, :], fresh_scores, -1e30)
    recent_score_peak, recent_weight_sum, fresh_weights = local_partial(fresh_scores)
    recent_output = jnp.einsum(
        "rtkgu,rukd->rtkgd", fresh_weights, recent_token_values, preferred_element_type=jnp.float32
    )
    partial_sets = []
    for step_index in range(step_count):
        query_all, member_all = (
            lax.all_gather(queries[:, step_index : step_index + 1], "req", axis=0, tiled=True),
            lax.all_gather(membership, "req", axis=0, tiled=True),
        )
        partial_sets.append(
            return_partials(
                *prefix_partials(
                    query_all,
                    member_all,
                    system_prefix_keys,
                    system_prefix_values,
                    kv_local,
                    score_scale,
                ),
                req_rows
            )
        )
    src_peak = jnp.concatenate([entry[0] for entry in partial_sets], axis=2)
    src_total = jnp.concatenate([entry[1] for entry in partial_sets], axis=2)
    src_out = jnp.concatenate([entry[2] for entry in partial_sets], axis=2)
    top_score = jnp.maximum(jnp.maximum(jnp.max(src_peak, axis=0), kept_peak), recent_score_peak)
    src_factor = jnp.exp(src_peak - top_score[None])
    kept_factor = jnp.exp(kept_peak - top_score)
    fresh_factor = jnp.exp(recent_score_peak - top_score)
    numerator = (
        jnp.sum(src_factor[..., None] * src_out, axis=0)
        + kept_factor[..., None] * kept_out
        + fresh_factor[..., None] * recent_output
    )
    denominator = (
        jnp.sum(src_factor * src_total, axis=0)
        + kept_factor * kept_total
        + fresh_factor * recent_weight_sum
    )
    attention = (
        (numerator / denominator[..., None])
        .astype(jnp.bfloat16)
        .reshape(req_rows, step_count, query_width)
    )
    piece_rows = lax.all_gather(attention, "req", axis=0, tiled=True)
    flat_rows = piece_rows.reshape(-1, query_width)
    partial_out = jnp.dot(flat_rows, out_weight, preferred_element_type=jnp.float32).reshape(
        piece_rows.shape[0], step_count, -1
    )
    return lax.psum(partial_out, "kvh").astype(jnp.bfloat16)


def solution(mesh):
    placed = (
        P("req", None, "kvh"),
        P("req", None, "kvh"),
        P("req", None, "kvh"),
        P(None, "req", "kvh"),
        P(None, "req", "kvh"),
        P("req", None, "kvh"),
        P("req", None, "kvh"),
        P("req", "kvh", None),
        P("req", None),
        P("kvh", "req"),
    )
    return jax.shard_map(
        local, mesh=mesh, in_specs=placed, out_specs=P(None, None, "req"), check_vma=False
    )
```

profile of v0, /device:TPU:0, one launch (start us, length us, event | category | flops | bytes accessed | tf_op | source)
XLA Modules:
  0.0 1125.0 jit_solution(11656335214572381754)
XLA Ops:
  9.2 20.6 %all-reduce = s32[64]{0:T(128)S(1)} all-reduce(s32[64]{0:T(128)S(1)} %bitcast_dynamic-update-slice_fusion), channel_id=1, replica_groups=mesh['req'=64,'kvh'=2] {'req'}, use_global_device_ids=true, to_apply=%add | all-reduce | flops 64 | bytes 512 | tf_op jit(solution)/shard_map/squeeze | solution.py:24
  35.8 79.2 %all_gather.22 = bf16[64,1,4096]{2,1,0:T(2,128)(2,1)S(1)} all-gather(bf16[1,1,4096]{2,1,0:T(2,128)(2,1)S(1)} %get-tuple-element.26), channel_id=1, replica_groups=mesh['req'=64,'kvh'=2] {'req'}, dimensions={0}, use_global_device_ids=true | all-gather | bytes 532480 | tf_op jit(solution)/shard_map/all_gather | solution.py:139
  115.0 3.3 reduce.71
  118.4 80.7 %all_gather.23 = bf16[64,1,4096]{2,1,0:T(2,128)(2,1)S(1)} all-gather(bf16[1,1,4096]{2,1,0:T(2,128)(2,1)S(1)} %get-tuple-element.28), channel_id=1, replica_groups=mesh['req'=64,'kvh'=2] {'req'}, dimensions={0}, use_global_device_ids=true | all-gather | bytes 532480 | tf_op jit(solution)/shard_map/all_gather | solution.py:139
  199.1 3.3 reduce.72
  208.0 79.4 %all_gather.24 = bf16[64,1,4096]{2,1,0:T(2,128)(2,1)S(1)} all-gather(bf16[1,1,4096]{2,1,0:T(2,128)(2,1)S(1)} %get-tuple-element.27), channel_id=1, replica_groups=mesh['req'=64,'kvh'=2] {'req'}, dimensions={0}, use_global_device_ids=true | all-gather | bytes 532480 | tf_op jit(solution)/shard_map/all_gather | solution.py:139
  287.4 4.1 reduce.73
  295.1 85.8 %all_gather.25 = bf16[64,1,4096]{2,1,0:T(2,128)(2,1)} all-gather(bf16[1,1,4096]{2,1,0:T(2,128)(2,1)S(1)} %get-tuple-element.29), channel_id=1, replica_groups=mesh['req'=64,'kvh'=2] {'req'}, dimensions={0}, use_global_device_ids=true | all-gather | bytes 532480 | tf_op jit(solution)/shard_map/all_gather | solution.py:139
  380.8 5.1 reduce.74
  426.1 2.7 fusion.409
  502.6 5.6 all-to-all-start.11
  508.2 2.9 fusion.408
  553.3 9.4 all-to-all-start.10
  585.0 9.3 all-to-all-start.9
  613.1 9.6 all-to-all-start.8
  640.6 9.3 all-to-all-start.3
  668.7 9.4 all-to-all-start.2
  690.9 9.0 all-to-all-start.1
  713.5 9.1 all-to-all-start
  748.2 9.7 all-to-all-start.7
  778.3 2.6 scatter_fusion.55
  787.2 9.9 all-to-all-start.6
  816.5 2.6 scatter_fusion.47
  823.7 9.5 all-to-all-start.5
  834.2 4.0 reshape.1933
  843.5 66.3 %gather_fusion.40 = bf16[4096,128]{1,0:T(8,128)(2,1)} fusion(bf16[1,2048,4,128]{3,2,1,0:T(4,128)(2,1)} %reshape.1933, s32[4096]{0:T(1024)S(1)} %reshape.2369), kind=kCustom, calls=%fused_computation.40 | custom fusion | bytes 2146304 | tf_op jit(solution)/shard_map/vmap()/gather | solution.py:100
  932.5 9.3 all-to-all-start.4
  944.7 40.2 %gather_fusion.41 = bf16[4096,128]{1,0:T(8,128)(2,1)} fusion(bf16[1,2048,4,128]{3,2,1,0:T(4,128)(2,1)S(1)} %reshape.1973, s32[4096]{0:T(1024)S(1)} %reshape.2369), kind=kCustom, calls=%fused_computation.41 | custom fusion | bytes 2146304 | tf_op jit(solution)/shard_map/vmap()/gather | solution.py:104
  990.9 3.6 fusion
  995.6 104.9 %all-gather.2.cloned.1.call-done = bf16[64,4,4096]{2,1,0:T(4,128)(2,1)} async-done(((bf16[1,4,4096]{2,1,0:T(4,128)(2,1)}), bf16[64,4,4096]{2,1,0:T(4,128)(2,1)}) %all-gather.2.cloned.1.call-update) | async-done | bytes 2097168 | tf_op jit(solution)/shard_map/all_gather | solution.py:177
  1100.5 4.1 fusion.1
  1104.6 12.7 %all-reduce.2 = bf16[64,4,128]{2,0,1:T(8,128)(2,1)S(1)} all-reduce(f32[64,4,128]{2,0,1:T(8,128)S(1)} %fusion.1), channel_id=1, replica_groups=mesh['req'=64,'kvh'=2] {'kvh'}, use_global_device_ids=true, to_apply=%region_170.171 | all-reduce | flops 32768 | bytes 196608 | tf_op jit(solution)/shard_map/psum | solution.py:182
  (954 shorter events, 388.6 us)
Async XLA Ops:
  6.5 1094.0 %copy-start = (bf16[4096,128]{1,0:T(8,128)(2,1)S(1)}, bf16[4096,128]{1,0:T(8,128)(2,1)}, u32[]{:S(2)}) copy-start(bf16[4096,128]{1,0:T(8,128)(2,1)} %param.19) | copy-start | bytes 3145732
  502.6 50.7 %all-to-all-start.11 = ((f32[64,1,32]{2,1,0:T(1,128)}), f32[64,1,32]{2,1,0:T(1,128)}, u32[]{:S(2)}, u32[]{:S(2)}) async-start(f32[64,1,32]{2,1,0:T(1,128)} %copy.1020), calls=%async_computation.11 | async-start | bytes 65536 | tf_op jit(solution)/shard_map/all_to_all | solution.py:69
  544.2 50.1 %copy-start.158 = (f32[16,4,8]{2,0,1:T(8,128)S(1)}, f32[16,4,8]{2,0,1:T(8,128)}, u32[]{:S(2)}) copy-start(f32[16,4,8]{2,0,1:T(8,128)} %copy-done.157) | copy-start | bytes 6148
  553.2 44.5 %copy-start.13 = (bf16[1,256,512]{1,2,0:T(8,128)(2,1)}, bf16[1,256,512]{1,2,0:T(8,128)(2,1)S(1)}, u32[]{:S(2)}) copy-start(bf16[1,256,512]{1,2,0:T(8,128)(2,1)S(1)} %copy.1241) | copy-start | bytes 786436
  553.2 43.2 %copy-start.181 = (f32[16,4,8]{2,0,1:T(8,128)S(1)}, f32[16,4,8]{2,0,1:T(8,128)}, u32[]{:S(2)}) copy-start(f32[16,4,8]{2,0,1:T(8,128)} %get-tuple-element.90) | copy-start | bytes 6148
  553.2 43.8 %copy-start.186 = (f32[16,4,8]{2,0,1:T(8,128)S(1)}, f32[16,4,8]{2,0,1:T(8,128)}, u32[]{:S(2)}) copy-start(f32[16,4,8]{2,0,1:T(8,128)} %get-tuple-element.82) | copy-start | bytes 6148
  553.2 44.4 %copy-start.190 = (f32[16,4,8]{2,0,1:T(8,128)S(1)}, f32[16,4,8]{2,0,1:T(8,128)}, u32[]{:S(2)}) copy-start(f32[16,4,8]{2,0,1:T(8,128)} %get-tuple-element.74) | copy-start | bytes 6148
  553.3 31.8 %all-to-all-start.10 = ((f32[64,1,32]{2,1,0:T(1,128)}), f32[64,1,32]{2,1,0:T(1,128)}, u32[]{:S(2)}, u32[]{:S(2)}) async-start(f32[64,1,32]{2,1,0:T(1,128)} %copy.1009), calls=%async_computation.10 | async-start | bytes 65536 | tf_op jit(solution)/shard_map/all_to_all | solution.py:69
  575.1 47.6 %copy-start.62 = (f32[16,1,4,8,256]{4,3,0,2,1:T(8,128)S(1)}, f32[16,1,4,8,256]{4,3,0,2,1:T(8,128)}, u32[]{:S(2)}) copy-start(f32[16,1,4,8,256]{4,3,0,2,1:T(8,128)} %copy-done.61) | copy-start | bytes 1572868
  575.2 47.6 %copy-start.154 = (f32[16,4,8]{2,0,1:T(8,128)S(1)}, f32[16,4,8]{2,0,1:T(8,128)}, u32[]{:S(2)}) copy-start(f32[16,4,8]{2,0,1:T(8,128)} %copy-done.153) | copy-start | bytes 6148
  585.0 28.0 %all-to-all-start.9 = ((f32[64,1,32]{2,1,0:T(1,128)}), f32[64,1,32]{2,1,0:T(1,128)}, u32[]{:S(2)}, u32[]{:S(2)}) async-start(f32[64,1,32]{2,1,0:T(1,128)} %copy.998), calls=%async_computation.9 | async-start | bytes 65536 | tf_op jit(solution)/shard_map/all_to_all | solution.py:69
  604.0 45.9 %copy-start.146 = (f32[16,4,8]{2,0,1:T(8,128)S(1)}, f32[16,4,8]{2,0,1:T(8,128)}, u32[]{:S(2)}) copy-start(f32[16,4,8]{2,0,1:T(8,128)} %copy-done.145) | copy-start | bytes 6148
  613.0 40.3 %copy-start.16 = (bf16[1,256,512]{1,2,0:T(8,128)(2,1)}, bf16[1,256,512]{1,2,0:T(8,128)(2,1)S(1)}, u32[]{:S(2)}) copy-start(bf16[1,256,512]{1,2,0:T(8,128)(2,1)S(1)} %copy.1242) | copy-start | bytes 786436
  613.0 39.6 %copy-start.175 = (f32[16,4,8]{2,0,1:T(8,128)S(1)}, f32[16,4,8]{2,0,1:T(8,128)}, u32[]{:S(2)}) copy-start(f32[16,4,8]{2,0,1:T(8,128)} %get-tuple-element.80) | copy-start | bytes 6148
  613.1 39.6 %copy-start.178 = (f32[16,4,8]{2,0,1:T(8,128)S(1)}, f32[16,4,8]{2,0,1:T(8,128)}, u32[]{:S(2)}) copy-start(f32[16,4,8]{2,0,1:T(8,128)} %get-tuple-element.72) | copy-start | bytes 6148
  613.1 40.2 %copy-start.183 = (f32[16,4,8]{2,0,1:T(8,128)S(1)}, f32[16,4,8]{2,0,1:T(8,128)}, u32[]{:S(2)}) copy-start(f32[16,4,8]{2,0,1:T(8,128)} %get-tuple-element.64) | copy-start | bytes 6148
  613.1 27.5 %all-to-all-start.8 = ((f32[64,1,32]{2,1,0:T(1,128)}), f32[64,1,32]{2,1,0:T(1,128)}, u32[]{:S(2)}, u32[]{:S(2)}) async-start(f32[64,1,32]{2,1,0:T(1,128)} %copy.987), calls=%async_computation.8 | async-start | bytes 65536 | tf_op jit(solution)/shard_map/all_to_all | solution.py:69
  630.7 47.4 %copy-start.55 = (f32[16,1,4,8,256]{4,3,0,2,1:T(8,128)S(1)}, f32[16,1,4,8,256]{4,3,0,2,1:T(8,128)}, u32[]{:S(2)}) copy-start(f32[16,1,4,8,256]{4,3,0,2,1:T(8,128)} %copy-done.54) | copy-start | bytes 1572868
  630.7 47.4 %copy-start.144 = (f32[16,4,8]{2,0,1:T(8,128)S(1)}, f32[16,4,8]{2,0,1:T(8,128)}, u32[]{:S(2)}) copy-start(f32[16,4,8]{2,0,1:T(8,128)} %copy-done.143) | copy-start | bytes 6148
  640.6 28.1 %all-to-all-start.3 = ((f32[64,1,32]{2,1,0:T(1,128)}), f32[64,1,32]{2,1,0:T(1,128)}, u32[]{:S(2)}, u32[]{:S(2)}) async-start(f32[64,1,32]{2,1,0:T(1,128)} %copy.881), calls=%async_computation.3 | async-start | bytes 65536 | tf_op jit(solution)/shard_map/all_to_all | solution.py:68
  659.1 40.8 %copy-start.138 = (f32[16,4,8]{2,0,1:T(8,128)S(1)}, f32[16,4,8]{2,0,1:T(8,128)}, u32[]{:S(2)}) copy-start(f32[16,4,8]{2,0,1:T(8,128)} %copy-done.137) | copy-start | bytes 6148
  668.7 22.2 %all-to-all-start.2 = ((f32[64,1,32]{2,1,0:T(1,128)}), f32[64,1,32]{2,1,0:T(1,128)}, u32[]{:S(2)}, u32[]{:S(2)}) async-start(f32[64,1,32]{2,1,0:T(1,128)} %copy.854), calls=%async_computation.2 | async-start | bytes 65536 | tf_op jit(solution)/shard_map/all_to_all | solution.py:68
  679.9 42.7 %copy-start.120 = (f32[16,4,8]{2,0,1:T(8,128)S(1)}, f32[16,4,8]{2,0,1:T(8,128)}, u32[]{:S(2)}) copy-start(f32[16,4,8]{2,0,1:T(8,128)} %copy-done.119) | copy-start | bytes 6148
  690.9 22.6 %all-to-all-start.1 = ((f32[64,1,32]{2,1,0:T(1,128)}), f32[64,1,32]{2,1,0:T(1,128)S(1)}, u32[]{:S(2)}, u32[]{:S(2)}) async-start(f32[64,1,32]{2,1,0:T(1,128)} %copy.827), calls=%async_computation.1 | async-start | bytes 65536 | tf_op jit(solution)/shard_map/all_to_all | solution.py:68
  713.5 34.8 %all-to-all-start = ((f32[64,1,32]{2,1,0:T(1,128)}), f32[64,1,32]{2,1,0:T(1,128)S(1)}, u32[]{:S(2)}, u32[]{:S(2)}) async-start(f32[64,1,32]{2,1,0:T(1,128)} %copy.800), calls=%async_computation | async-start | bytes 65536 | tf_op jit(solution)/shard_map/all_to_all | solution.py:68
  748.2 38.9 %all-to-all-start.7 = ((f32[64,1,4096]{2,1,0:T(1,128)}), f32[64,1,4096]{2,1,0:T(1,128)}, u32[]{:S(2)}, u32[]{:S(2)}) async-start(f32[64,1,4096]{2,1,0:T(1,128)} %bitcast.538), calls=%async_computation.7 | async-start | bytes 2097152 | tf_op jit(solution)/shard_map/all_to_all | solution.py:67
  787.2 36.5 %all-to-all-start.6 = ((f32[64,1,4096]{2,1,0:T(1,128)}), f32[64,1,4096]{2,1,0:T(1,128)}, u32[]{:S(2)}, u32[]{:S(2)}) async-start(f32[64,1,4096]{2,1,0:T(1,128)} %bitcast.472), calls=%async_computation.6 | async-start | bytes 2097152 | tf_op jit(solution)/shard_map/all_to_all | solution.py:67
  823.7 108.8 %all-to-all-start.5 = ((f32[64,1,4096]{2,1,0:T(1,128)}), f32[64,1,4096]{2,1,0:T(1,128)}, u32[]{:S(2)}, u32[]{:S(2)}) async-start(f32[64,1,4096]{2,1,0:T(1,128)} %bitcast.406), calls=%async_computation.5 | async-start | bytes 2097152 | tf_op jit(solution)/shard_map/all_to_all | solution.py:67
  932.5 58.5 %all-to-all-start.4 = ((f32[64,1,4096]{2,1,0:T(1,128)}), f32[64,1,4096]{2,1,0:T(1,128)}, u32[]{:S(2)}, u32[]{:S(2)}) async-start(f32[64,1,4096]{2,1,0:T(1,128)} %bitcast.340), calls=%async_computation.4 | async-start | bytes 2097152 | tf_op jit(solution)/shard_map/all_to_all | solution.py:67
  941.8 158.8 %all-gather.2.cloned.1.call-start = ((), (), s32[]{:S(2)}) async-start(), calls=%async_computation.12 | async-start | bytes 2129920 | tf_op jit(solution)/shard_map/all_gather | solution.py:177
  944.6 45.2 %copy-start.206 = (f32[64,1,32]{2,1,0:T(1,128)S(1)}, f32[64,1,32]{2,1,0:T(1,128)}, u32[]{:S(2)}) copy-start(f32[64,1,32]{2,1,0:T(1,128)} %copy-done.205) | copy-start | bytes 24580
  944.7 46.0 %copy-start.243 = (bf16[1,4,512]{2,1,0:T(4,128)(2,1)S(1)}, bf16[1,4,512]{2,1,0:T(4,128)(2,1)}, u32[]{:S(2)}) copy-start(bf16[1,4,512]{2,1,0:T(4,128)(2,1)} %param.12) | copy-start | bytes 12292
  (225 other events, 1733.3 us)
Sparse Core Ops, SparseCore 0:
  995.7 104.7 all-gather.1
where the time goes:
time: 1140 us; the launch traced here: 1130 us
  blocking collectives  358 us (31%)
  local copies, waits for them, and re-layouts  245 us (21%)
  other arithmetic  205 us (18%)
  starting transfers between devices  109 us (10%)
  waiting for transfers between devices  105 us (9%)
  matrix products  83.1 us (7%)
  between operations  19.2 us (2%)
    all_gather x4, blocking collectives, local(): lax.all_gather(queries[:, step_index:step_index + 1], 'req', axis=0, tile...  325 us
    all_gather x1, waiting for transfers between devices, local(): piece_rows = lax.all_gather(attention, 'req', axis=0, tiled=True)  105 us
    scatter-add x32, other arithmetic, prefix_partials(): out_all.at[slot_rows].add(jnp.where(is_valid[..., None], part_out, 0.0))  78.6 us
    gather x4, local copies, waits for them, and re-layouts, local(): key_table[pick_list.T, head_index_list]  66.8 us
    dot_general x32, matrix products, prefix_partials(): jnp.einsum('cskgl,lkd->cskgd', weights, stretch_values, preferred_element...  44.8 us
    gather x1, local copies, waits for them, and re-layouts, local(): value_table[pick_list.T, head_index_list]  40.2 us
    scatter-add x32, other arithmetic, prefix_partials(): total_all = total_all.at[slot_rows].add(jnp.where(is_valid, row_total, 0.0))  39.9 us
    scatter-add x32, other arithmetic, prefix_partials(): peak_all = peak_all.at[slot_rows].add(jnp.where(is_valid, row_peak, 0.0))  39.9 us
  transfers between devices with their start and end apart: 13, of which 1 were waited for; matrix products, arithmetic and copies ran while one was open for 33% of the time, Pallas kernels for 0%

commit v1 on v0

--- a/solution.py
+++ b/solution.py
@@ -6,6 +6,13 @@
 HEAD_WIDTH = 128
 HEADS_PER_GROUP = 8
 PROMPT_COUNT = 8
+
+
+def swapped_in(value, mesh_axis, d):
+    size = lax.axis_size(mesh_axis)
+    blocks = jnp.stack([value for _ in range(size)])
+    blocks = lax.all_to_all(blocks, mesh_axis, split_axis=0, concat_axis=0)
+    return jnp.concatenate(blocks, axis=d)
 
 
 def local_partial(scores):
@@ -136,7 +143,7 @@
     partial_sets = []
     for step_index in range(step_count):
         query_all, member_all = (
-            lax.all_gather(queries[:, step_index : step_index + 1], "req", axis=0, tiled=True),
+            swapped_in(queries[:, step_index : step_index + 1], "req", 0),
             lax.all_gather(membership, "req", axis=0, tiled=True),
         )
         partial_sets.append(

time: 1140 us -> 892 us (0.78)
  blocking collectives: 358 us -> 32.9 us
  matrix products: 83.1 us -> 43.5 us
  other arithmetic: 205 us -> 240 us
  local copies, waits for them, and re-layouts: 245 us -> 277 us
  starting transfers between devices: 109 us -> 138 us
  waiting for transfers between devices: 105 us -> 126 us
    all_gather x4 -> x0, blocking collectives: 325 us -> none  [local(): lax.all_gather(queries[:, step_index:step_index + 1], 'req', axis=0, tile...]
    all_to_all x0 -> x4, starting transfers between devices: none -> 24.8 us  [swapped_in(): blocks = lax.all_to_all(blocks, mesh_axis, split_axis=0, concat_axis=0)]
    unnamed x511 -> x535, local copies, waits for them, and re-layouts: 22.4 us -> 47.2 us
    gather x4, local copies, waits for them, and re-layouts: 66.8 us -> 42.5 us  [local(): key_table[pick_list.T, head_index_list]]
    all_to_all x0 -> x4, waiting for transfers between devices: none -> 21.3 us  [swapped_in(): blocks = lax.all_to_all(blocks, mesh_axis, split_axis=0, concat_axis=0)]
    dot_general x32, matrix products: 32.9 us -> 11.6 us  [prefix_partials(): jnp.einsum('cskgd,lkd->cskgl', chosen_index, stretch_keys, preferred_elem...]
    dot_general x32, matrix products: 44.8 us -> 25.3 us  [prefix_partials(): jnp.einsum('cskgl,lkd->cskgd', weights, stretch_values, preferred_element...]
    select_n x32, local copies, waits for them, and re-layouts: 10.9 us -> 28.4 us  [prefix_partials(): peak_all = peak_all.at[slot_rows].add(jnp.where(is_valid, row_peak, 0.0))]
  transfers between devices with their start and end apart: 13 -> 17, of which waited for: 1 -> 3; matrix products, arithmetic and copies ran while one was open for 33% -> 51% of each run, Pallas kernels for 0% -> 0%
where the time goes in v1:
time: 892 us; the launch traced here: 876 us
  local copies, waits for them, and re-layouts  277 us (31%)
  other arithmetic  240 us (27%)
  starting transfers between devices  138 us (15%)
  waiting for transfers between devices  126 us (14%)
  matrix products  43.5 us (5%)
  blocking collectives  32.9 us (4%)
  between operations  19.2 us (2%)
    all_gather x1, waiting for transfers between devices, local(): piece_rows = lax.all_gather(attention, 'req', axis=0, tiled=True)  105 us
    scatter-add x32, other arithmetic, prefix_partials(): out_all.at[slot_rows].add(jnp.where(is_valid[..., None], part_out, 0.0))  79.1 us
    scatter-add x32, other arithmetic, prefix_partials(): total_all = total_all.at[slot_rows].add(jnp.where(is_valid, row_total, 0.0))  49.3 us
    unnamed x535, local copies, waits for them, and re-layouts  47.2 us
    scatter-add x32, other arithmetic, prefix_partials(): peak_all = peak_all.at[slot_rows].add(jnp.where(is_valid, row_peak, 0.0))  44.9 us
    gather x4, local copies, waits for them, and re-layouts, local(): key_table[pick_list.T, head_index_list]  42.5 us
    gather x32, local copies, waits for them, and re-layouts, prefix_partials(): chosen_index = grouped_query_heads[slot_rows]  41 us
    gather x1, local copies, waits for them, and re-layouts, local(): value_table[pick_list.T, head_index_list]  40.1 us
  transfers between devices with their start and end apart: 17, of which 3 were waited for; matrix products, arithmetic and copies ran while one was open for 51% of the time, Pallas kernels for 0%

profile of v1, /device:TPU:0, one launch (start us, length us, event | category | flops | bytes accessed | tf_op | source)
XLA Modules:
  0.0 876.1 jit_solution(17478132950932574918)
XLA Ops:
  9.2 4.6 reduce.83
  16.1 9.7 %all-to-all-start = ((bf16[64,2,2048]{2,1,0:T(2,128)(2,1)}), bf16[64,2,2048]{2,1,0:T(2,128)(2,1)}, u32[]{:S(2)}, u32[]{:S(2)}) async-start(bf16[64,2,2048]{2,1,0:T(2,128)(2,1)} %reshape.3592), calls=%async_computation | async-start | bytes 1048576 | tf_op jit(solution)/shard_map/all_to_all | solution.py:14
  27.7 20.2 %all-reduce = s32[64]{0:T(128)S(1)} all-reduce(s32[64]{0:T(128)S(1)} %bitcast_dynamic-update-slice_fusion), channel_id=1, replica_groups=mesh['req'=64,'kvh'=2] {'req'}, use_global_device_ids=true, to_apply=%add | all-reduce | flops 64 | bytes 512 | tf_op jit(solution)/shard_map/squeeze | solution.py:31
  58.2 3.8 reduce.84
  64.2 3.8 reduce.85
  70.2 4.0 reduce.86
  117.8 40.2 %gather_fusion.40 = bf16[4096,128]{1,0:T(8,128)(2,1)} fusion(bf16[1,2048,4,128]{3,2,1,0:T(4,128)(2,1)S(1)} %reshape.1929, s32[4096]{0:T(1024)S(1)} %reshape.2365), kind=kCustom, calls=%fused_computation.40 | custom fusion | bytes 2146304 | tf_op jit(solution)/shard_map/vmap()/gather | solution.py:107
  159.3 4.6 all-to-all-start.2
  164.5 11.3 %all-to-all-done.2 = bf16[64,2,2048]{2,1,0:T(2,128)(2,1)S(1)} async-done(((bf16[64,2,2048]{2,1,0:T(2,128)(2,1)}), bf16[64,2,2048]{2,1,0:T(2,128)(2,1)S(1)}, u32[]{:S(2)}, u32[]{:S(2)}) %all-to-all-start.2) | async-done | bytes 524320 | tf_op jit(solution)/shard_map/all_to_all | solution.py:14
  175.8 4.6 all-to-all-start.4
  182.3 10.0 %all-to-all-done.4 = bf16[64,2,2048]{2,1,0:T(2,128)(2,1)S(1)} async-done(((bf16[64,2,2048]{2,1,0:T(2,128)(2,1)}), bf16[64,2,2048]{2,1,0:T(2,128)(2,1)S(1)}, u32[]{:S(2)}, u32[]{:S(2)}) %all-to-all-start.4) | async-done | bytes 524320 | tf_op jit(solution)/shard_map/all_to_all | solution.py:14
  192.3 5.9 all-to-all-start.6
  201.1 3.6 reshape.3593
  220.3 3.9 reduce.76
  227.8 4.6 reshape.3587
  232.4 5.1 reduce.78
  318.7 9.7 %all-to-all-start.15 = ((f32[64,1,32]{2,1,0:T(1,128)}), f32[64,1,32]{2,1,0:T(1,128)}, u32[]{:S(2)}, u32[]{:S(2)}) async-start(f32[64,1,32]{2,1,0:T(1,128)} %copy.1020), calls=%async_computation.15 | async-start | bytes 65536 | tf_op jit(solution)/shard_map/all_to_all | solution.py:76
  349.5 9.3 %all-to-all-start.14 = ((f32[64,1,32]{2,1,0:T(1,128)}), f32[64,1,32]{2,1,0:T(1,128)}, u32[]{:S(2)}, u32[]{:S(2)}) async-start(f32[64,1,32]{2,1,0:T(1,128)} %copy.1009), calls=%async_computation.14 | async-start | bytes 65536 | tf_op jit(solution)/shard_map/all_to_all | solution.py:76
  383.4 9.3 %all-to-all-start.13 = ((f32[64,1,32]{2,1,0:T(1,128)}), f32[64,1,32]{2,1,0:T(1,128)}, u32[]{:S(2)}, u32[]{:S(2)}) async-start(f32[64,1,32]{2,1,0:T(1,128)} %copy.998), calls=%async_computation.13 | async-start | bytes 65536 | tf_op jit(solution)/shard_map/all_to_all | solution.py:76
  421.1 9.3 %all-to-all-start.12 = ((f32[64,1,32]{2,1,0:T(1,128)}), f32[64,1,32]{2,1,0:T(1,128)}, u32[]{:S(2)}, u32[]{:S(2)}) async-start(f32[64,1,32]{2,1,0:T(1,128)} %copy.987), calls=%async_computation.12 | async-start | bytes 65536 | tf_op jit(solution)/shard_map/all_to_all | solution.py:76
  458.9 9.3 %all-to-all-start.7 = ((f32[64,1,32]{2,1,0:T(1,128)}), f32[64,1,32]{2,1,0:T(1,128)}, u32[]{:S(2)}, u32[]{:S(2)}) async-start(f32[64,1,32]{2,1,0:T(1,128)} %copy.881), calls=%async_computation.7 | async-start | bytes 65536 | tf_op jit(solution)/shard_map/all_to_all | solution.py:75
  496.6 9.3 %all-to-all-start.5 = ((f32[64,1,32]{2,1,0:T(1,128)}), f32[64,1,32]{2,1,0:T(1,128)}, u32[]{:S(2)}, u32[]{:S(2)}) async-start(f32[64,1,32]{2,1,0:T(1,128)} %copy.854), calls=%async_computation.5 | async-start | bytes 65536 | tf_op jit(solution)/shard_map/all_to_all | solution.py:75
  524.1 9.5 %all-to-all-start.3 = ((f32[64,1,32]{2,1,0:T(1,128)}), f32[64,1,32]{2,1,0:T(1,128)}, u32[]{:S(2)}, u32[]{:S(2)}) async-start(f32[64,1,32]{2,1,0:T(1,128)} %copy.827), calls=%async_computation.3 | async-start | bytes 65536 | tf_op jit(solution)/shard_map/all_to_all | solution.py:75
  545.7 9.0 %all-to-all-start.1 = ((f32[64,1,32]{2,1,0:T(1,128)}), f32[64,1,32]{2,1,0:T(1,128)S(1)}, u32[]{:S(2)}, u32[]{:S(2)}) async-start(f32[64,1,32]{2,1,0:T(1,128)} %copy.800), calls=%async_computation.1 | async-start | bytes 65536 | tf_op jit(solution)/shard_map/all_to_all | solution.py:75
  580.8 9.5 %all-to-all-start.11 = ((f32[64,1,4096]{2,1,0:T(1,128)}), f32[64,1,4096]{2,1,0:T(1,128)}, u32[]{:S(2)}, u32[]{:S(2)}) async-start(f32[64,1,4096]{2,1,0:T(1,128)} %bitcast.538), calls=%async_computation.11 | async-start | bytes 2097152 | tf_op jit(solution)/shard_map/all_to_all | solution.py:74
  614.8 9.6 %all-to-all-start.10 = ((f32[64,1,4096]{2,1,0:T(1,128)}), f32[64,1,4096]{2,1,0:T(1,128)}, u32[]{:S(2)}, u32[]{:S(2)}) async-start(f32[64,1,4096]{2,1,0:T(1,128)} %bitcast.472), calls=%async_computation.10 | async-start | bytes 2097152 | tf_op jit(solution)/shard_map/all_to_all | solution.py:74
  648.7 9.7 %all-to-all-start.9 = ((f32[64,1,4096]{2,1,0:T(1,128)}), f32[64,1,4096]{2,1,0:T(1,128)}, u32[]{:S(2)}, u32[]{:S(2)}) async-start(f32[64,1,4096]{2,1,0:T(1,128)} %bitcast.406), calls=%async_computation.9 | async-start | bytes 2097152 | tf_op jit(solution)/shard_map/all_to_all | solution.py:74
  682.5 9.4 %all-to-all-start.8 = ((f32[64,1,4096]{2,1,0:T(1,128)}), f32[64,1,4096]{2,1,0:T(1,128)}, u32[]{:S(2)}, u32[]{:S(2)}) async-start(f32[64,1,4096]{2,1,0:T(1,128)} %bitcast.340), calls=%async_computation.8 | async-start | bytes 2097152 | tf_op jit(solution)/shard_map/all_to_all | solution.py:74
  695.0 40.1 %gather_fusion.41 = bf16[4096,128]{1,0:T(8,128)(2,1)} fusion(bf16[1,2048,4,128]{3,2,1,0:T(4,128)(2,1)S(1)} %reshape.1969, s32[4096]{0:T(1024)S(1)} %copy-done.2), kind=kCustom, calls=%fused_computation.41 | custom fusion | bytes 2146304 | tf_op jit(solution)/shard_map/vmap()/gather | solution.py:111
  746.6 104.9 %all-gather.2.cloned.1.call-done = bf16[64,4,4096]{2,1,0:T(4,128)(2,1)} async-done(((bf16[1,4,4096]{2,1,0:T(4,128)(2,1)}), bf16[64,4,4096]{2,1,0:T(4,128)(2,1)}) %all-gather.2.cloned.1.call-update) | async-done | bytes 2097168 | tf_op jit(solution)/shard_map/all_gather | solution.py:184
  851.6 4.1 fusion.1
  855.6 12.7 %all-reduce.2 = bf16[64,4,128]{2,0,1:T(8,128)(2,1)S(1)} all-reduce(f32[64,4,128]{2,0,1:T(8,128)S(1)} %fusion.1), channel_id=1, replica_groups=mesh['req'=64,'kvh'=2] {'kvh'}, use_global_device_ids=true, to_apply=%region_170.171 | all-reduce | flops 32768 | bytes 196608 | tf_op jit(solution)/shard_map/psum | solution.py:189
  (991 shorter events, 442.4 us)
Async XLA Ops:
  6.5 845.0 %copy-start = (bf16[4096,128]{1,0:T(8,128)(2,1)S(1)}, bf16[4096,128]{1,0:T(8,128)(2,1)}, u32[]{:S(2)}) copy-start(bf16[4096,128]{1,0:T(8,128)(2,1)} %param.19) | copy-start | bytes 3145732
  16.1 143.2 %all-to-all-start = ((bf16[64,2,2048]{2,1,0:T(2,128)(2,1)}), bf16[64,2,2048]{2,1,0:T(2,128)(2,1)}, u32[]{:S(2)}, u32[]{:S(2)}) async-start(bf16[64,2,2048]{2,1,0:T(2,128)(2,1)} %reshape.3592), calls=%async_computation | async-start | bytes 1048576 | tf_op jit(solution)/shard_map/all_to_all | solution.py:14
  117.8 436.9 %copy-start.4 = (bf16[1,256,512]{1,2,0:T(8,128)(2,1)}, bf16[1,256,512]{1,2,0:T(8,128)(2,1)S(1)}, u32[]{:S(2)}) copy-start(bf16[1,256,512]{1,2,0:T(8,128)(2,1)S(1)} %copy.1243) | copy-start | bytes 786436
  157.9 40.3 %copy-start.107 = (bf16[4096,128]{1,0:T(8,128)(2,1)S(1)}, bf16[4096,128]{1,0:T(8,128)(2,1)}, u32[]{:S(2)}) copy-start(bf16[4096,128]{1,0:T(8,128)(2,1)} %gather_fusion.40) | copy-start | bytes 3145732
  157.9 40.3 %copy-start.215 = (bf16[1,4,4096]{2,1,0:T(4,128)(2,1)S(1)}, bf16[1,4,4096]{2,1,0:T(4,128)(2,1)}, u32[]{:S(2)}) copy-start(bf16[1,4,4096]{2,1,0:T(4,128)(2,1)} %param.10) | copy-start | bytes 98308
  159.3 16.5 %all-to-all-start.2 = ((bf16[64,2,2048]{2,1,0:T(2,128)(2,1)}), bf16[64,2,2048]{2,1,0:T(2,128)(2,1)S(1)}, u32[]{:S(2)}, u32[]{:S(2)}) async-start(bf16[64,2,2048]{2,1,0:T(2,128)(2,1)} %reshape.3590), calls=%async_computation.2 | async-start | bytes 1048576 | tf_op jit(solution)/shard_map/all_to_all | solution.py:14
  175.8 16.5 %all-to-all-start.4 = ((bf16[64,2,2048]{2,1,0:T(2,128)(2,1)}), bf16[64,2,2048]{2,1,0:T(2,128)(2,1)S(1)}, u32[]{:S(2)}, u32[]{:S(2)}) async-start(bf16[64,2,2048]{2,1,0:T(2,128)(2,1)} %reshape.3588), calls=%async_computation.4 | async-start | bytes 1048576 | tf_op jit(solution)/shard_map/all_to_all | solution.py:14
  192.3 35.5 %all-to-all-start.6 = ((bf16[64,2,2048]{2,1,0:T(2,128)(2,1)}), bf16[64,2,2048]{2,1,0:T(2,128)(2,1)}, u32[]{:S(2)}, u32[]{:S(2)}) async-start(bf16[64,2,2048]{2,1,0:T(2,128)(2,1)} %reshape.3586), calls=%async_computation.6 | async-start | bytes 1048576 | tf_op jit(solution)/shard_map/all_to_all | solution.py:14
  316.6 42.2 %copy-start.24 = (bf16[1,256,512]{1,2,0:T(8,128)(2,1)S(1)}, bf16[1,256,512]{1,2,0:T(8,128)(2,1)}, u32[]{:S(2)}) copy-start(bf16[1,256,512]{1,2,0:T(8,128)(2,1)} %copy.1238) | copy-start | bytes 786436
  317.3 41.5 %copy-start.187 = (f32[16,4,8]{2,0,1:T(8,128)S(1)}, f32[16,4,8]{2,0,1:T(8,128)}, u32[]{:S(2)}) copy-start(f32[16,4,8]{2,0,1:T(8,128)} %copy-done.186) | copy-start | bytes 6148
  318.7 30.8 %all-to-all-start.15 = ((f32[64,1,32]{2,1,0:T(1,128)}), f32[64,1,32]{2,1,0:T(1,128)}, u32[]{:S(2)}, u32[]{:S(2)}) async-start(f32[64,1,32]{2,1,0:T(1,128)} %copy.1020), calls=%async_computation.15 | async-start | bytes 65536 | tf_op jit(solution)/shard_map/all_to_all | solution.py:76
  349.5 34.0 %all-to-all-start.14 = ((f32[64,1,32]{2,1,0:T(1,128)}), f32[64,1,32]{2,1,0:T(1,128)}, u32[]{:S(2)}, u32[]{:S(2)}) async-start(f32[64,1,32]{2,1,0:T(1,128)} %copy.1009), calls=%async_computation.14 | async-start | bytes 65536 | tf_op jit(solution)/shard_map/all_to_all | solution.py:76
  363.9 66.5 %copy-start.20 = (bf16[1,256,512]{1,2,0:T(8,128)(2,1)S(1)}, bf16[1,256,512]{1,2,0:T(8,128)(2,1)}, u32[]{:S(2)}) copy-start(bf16[1,256,512]{1,2,0:T(8,128)(2,1)} %copy.1239) | copy-start | bytes 786436
  383.4 37.7 %all-to-all-start.13 = ((f32[64,1,32]{2,1,0:T(1,128)}), f32[64,1,32]{2,1,0:T(1,128)}, u32[]{:S(2)}, u32[]{:S(2)}) async-start(f32[64,1,32]{2,1,0:T(1,128)} %copy.998), calls=%async_computation.13 | async-start | bytes 65536 | tf_op jit(solution)/shard_map/all_to_all | solution.py:76
  401.6 66.6 %copy-start.16 = (bf16[1,256,512]{1,2,0:T(8,128)(2,1)S(1)}, bf16[1,256,512]{1,2,0:T(8,128)(2,1)}, u32[]{:S(2)}) copy-start(bf16[1,256,512]{1,2,0:T(8,128)(2,1)} %copy.1240) | copy-start | bytes 786436
  421.1 37.7 %all-to-all-start.12 = ((f32[64,1,32]{2,1,0:T(1,128)}), f32[64,1,32]{2,1,0:T(1,128)}, u32[]{:S(2)}, u32[]{:S(2)}) async-start(f32[64,1,32]{2,1,0:T(1,128)} %copy.987), calls=%async_computation.12 | async-start | bytes 65536 | tf_op jit(solution)/shard_map/all_to_all | solution.py:76
  439.3 66.6 %copy-start.12 = (bf16[1,256,512]{1,2,0:T(8,128)(2,1)S(1)}, bf16[1,256,512]{1,2,0:T(8,128)(2,1)}, u32[]{:S(2)}) copy-start(bf16[1,256,512]{1,2,0:T(8,128)(2,1)} %copy.1241) | copy-start | bytes 786436
  458.9 37.8 %all-to-all-start.7 = ((f32[64,1,32]{2,1,0:T(1,128)}), f32[64,1,32]{2,1,0:T(1,128)}, u32[]{:S(2)}, u32[]{:S(2)}) async-start(f32[64,1,32]{2,1,0:T(1,128)} %copy.881), calls=%async_computation.7 | async-start | bytes 65536 | tf_op jit(solution)/shard_map/all_to_all | solution.py:75
  477.1 56.5 %copy-start.8 = (bf16[1,256,512]{1,2,0:T(8,128)(2,1)S(1)}, bf16[1,256,512]{1,2,0:T(8,128)(2,1)}, u32[]{:S(2)}) copy-start(bf16[1,256,512]{1,2,0:T(8,128)(2,1)} %copy.1242) | copy-start | bytes 786436
  495.2 40.1 %copy-start.192 = (f32[16,4,8]{2,0,1:T(8,128)S(1)}, f32[16,4,8]{2,0,1:T(8,128)}, u32[]{:S(2)}) copy-start(f32[16,4,8]{2,0,1:T(8,128)} %get-tuple-element.70) | copy-start | bytes 6148
  496.6 27.4 %all-to-all-start.5 = ((f32[64,1,32]{2,1,0:T(1,128)}), f32[64,1,32]{2,1,0:T(1,128)}, u32[]{:S(2)}, u32[]{:S(2)}) async-start(f32[64,1,32]{2,1,0:T(1,128)} %copy.854), calls=%async_computation.5 | async-start | bytes 65536 | tf_op jit(solution)/shard_map/all_to_all | solution.py:75
  511.6 43.1 %copy-start.179 = (f32[16,4,8]{2,0,1:T(8,128)S(1)}, f32[16,4,8]{2,0,1:T(8,128)}, u32[]{:S(2)}) copy-start(f32[16,4,8]{2,0,1:T(8,128)} %copy-done.178) | copy-start | bytes 6148
  524.1 21.6 %all-to-all-start.3 = ((f32[64,1,32]{2,1,0:T(1,128)}), f32[64,1,32]{2,1,0:T(1,128)}, u32[]{:S(2)}, u32[]{:S(2)}) async-start(f32[64,1,32]{2,1,0:T(1,128)} %copy.827), calls=%async_computation.3 | async-start | bytes 65536 | tf_op jit(solution)/shard_map/all_to_all | solution.py:75
  545.7 35.1 %all-to-all-start.1 = ((f32[64,1,32]{2,1,0:T(1,128)}), f32[64,1,32]{2,1,0:T(1,128)S(1)}, u32[]{:S(2)}, u32[]{:S(2)}) async-start(f32[64,1,32]{2,1,0:T(1,128)} %copy.800), calls=%async_computation.1 | async-start | bytes 65536 | tf_op jit(solution)/shard_map/all_to_all | solution.py:75
  580.8 34.0 %all-to-all-start.11 = ((f32[64,1,4096]{2,1,0:T(1,128)}), f32[64,1,4096]{2,1,0:T(1,128)}, u32[]{:S(2)}, u32[]{:S(2)}) async-start(f32[64,1,4096]{2,1,0:T(1,128)} %bitcast.538), calls=%async_computation.11 | async-start | bytes 2097152 | tf_op jit(solution)/shard_map/all_to_all | solution.py:74
  614.8 33.8 %all-to-all-start.10 = ((f32[64,1,4096]{2,1,0:T(1,128)}), f32[64,1,4096]{2,1,0:T(1,128)}, u32[]{:S(2)}, u32[]{:S(2)}) async-start(f32[64,1,4096]{2,1,0:T(1,128)} %bitcast.472), calls=%async_computation.10 | async-start | bytes 2097152 | tf_op jit(solution)/shard_map/all_to_all | solution.py:74
  648.7 33.9 %all-to-all-start.9 = ((f32[64,1,4096]{2,1,0:T(1,128)}), f32[64,1,4096]{2,1,0:T(1,128)}, u32[]{:S(2)}, u32[]{:S(2)}) async-start(f32[64,1,4096]{2,1,0:T(1,128)} %bitcast.406), calls=%async_computation.9 | async-start | bytes 2097152 | tf_op jit(solution)/shard_map/all_to_all | solution.py:74
  682.5 59.4 %all-to-all-start.8 = ((f32[64,1,4096]{2,1,0:T(1,128)}), f32[64,1,4096]{2,1,0:T(1,128)}, u32[]{:S(2)}, u32[]{:S(2)}) async-start(f32[64,1,4096]{2,1,0:T(1,128)} %bitcast.340), calls=%async_computation.8 | async-start | bytes 2097152 | tf_op jit(solution)/shard_map/all_to_all | solution.py:74
  691.9 159.6 %all-gather.2.cloned.1.call-start = ((), (), s32[]{:S(2)}) async-start(), calls=%async_computation.16 | async-start | bytes 2129920 | tf_op jit(solution)/shard_map/all_gather | solution.py:184
  694.9 46.2 %copy-start.225 = (f32[4,4,8]{2,0,1:T(4,128)S(1)}, f32[4,4,8]{2,0,1:T(4,128)}, u32[]{:S(2)}) copy-start(f32[4,4,8]{2,0,1:T(4,128)} %copy-done.224) | copy-start | bytes 1540
  694.9 46.4 %copy-start.227 = (f32[4,4,8]{2,0,1:T(4,128)S(1)}, f32[4,4,8]{2,0,1:T(4,128)}, u32[]{:S(2)}) copy-start(f32[4,4,8]{2,0,1:T(4,128)} %fusion.175) | copy-start | bytes 1540
  695.0 46.8 %copy-start.250 = (bf16[1,4,512]{2,1,0:T(4,128)(2,1)S(1)}, bf16[1,4,512]{2,1,0:T(4,128)(2,1)}, u32[]{:S(2)}) copy-start(bf16[1,4,512]{2,1,0:T(4,128)(2,1)} %param.12) | copy-start | bytes 12292
  (237 other events, 1518.2 us)
Sparse Core Ops, SparseCore 0:
  746.8 104.7 all-gather.1
